TPU v7x, 128 devices: a whole 4x4x4 slice. The times are simulated.
128 devices in a mesh: ctx: 64 (over z, x, y), head: 2 (over core).
Axes of the slice: x: 4, y: 4, z: 4, core: 2. Of those that a mesh axis runs over, the one named last changes fastest.
Arguments:
- queries: bfloat16 [16384, 2048], P('ctx', 'head'), may hold values from -6 to 6
- keys: bfloat16 [16384, 2048], P('ctx', 'head'), may hold values from -6 to 6
- values: bfloat16 [16384, 2048], P('ctx', 'head'), may hold values from -6 to 6
- out_weight: bfloat16 [2048, 2048], P('head'), may hold values from -0.125 to 0.125
- grad_out: bfloat16 [16384, 2048], P('ctx', 'head'), may hold values from -16 to 16
- doc_ids: int32 [16384], P('ctx'), may hold values from 0 to 3, never falling along the last dimension, each value on 1 to 8192 neighbouring positions
Outputs:
- grad_queries: bfloat16 [16384, 2048], P('ctx', 'head')
- grad_keys: bfloat16 [16384, 2048], P('ctx', 'head')
- grad_values: bfloat16 [16384, 2048], P('ctx', 'head')
- grad_weight: float32 [2048, 16, 128], P('ctx', 'head')
Inputs may be any that keep to these rules, and one draw needn't show every extreme that they name: `doc_ids`: document numbers never fall along the sequence and start at 0; all 4 documents occur, each 1 to 8192 positions long, one exactly 8192.
All inputs are finite; a program needn't handle non-finite values.
Results may differ from a plain program's by a relative error of at most 0.018.
Values may be sent and summed in bfloat16 or wider, within the bound.
A program may use at most 192 MiB of HBM per device.

v0:
```python
import math

import jax
import jax.numpy as jnp
from jax import lax
from jax.sharding import PartitionSpec as P

HD = 128
DOCS = 4


def prefix(array, axis, join, neutral, backward):
    count = lax.axis_size(axis)
    place = lax.axis_index(axis)
    ahead = count - 1 - place if backward else place
    gathered = jax.tree.map(
        lambda a, kind: lax.all_gather(a.astype(kind), axis), array, (jnp.bfloat16, jnp.int32)
    )
    state = jax.tree.map(lambda a, e: jnp.zeros_like(a) + jnp.asarray(e, a.dtype), array, neutral)

    def one(step, state):
        source = count - 1 - step if backward else step
        return join(
            state,
            jax.tree.map(
                lambda a, own: lax.dynamic_index_in_dim(a, source, 0, False).astype(own.dtype),
                gathered,
                array,
            ),
        )

    return lax.fori_loop(0, ahead, one, state)


def exact_product(form, left, right):
    return jnp.einsum(
        form, left.astype(jnp.float32), right.astype(jnp.float32), precision=lax.Precision.HIGHEST
    )


def chain_link(earlier_part, later_part):
    earlier_states, earlier_mark = earlier_part
    later_states, later_mark = later_part
    joined = (later_mark < 0) | (earlier_mark == later_mark)
    merged = later_states + jnp.where(joined, earlier_states, jnp.zeros_like(earlier_states))
    return (merged, jnp.where(later_mark < 0, earlier_mark, later_mark))


def block_terms(pieces):
    query_block, key_block, value_block, grad_block, id_block = pieces
    places = lax.iota(jnp.int32, id_block.shape[0])
    allowed = (places[:, None] >= places[None, :]) & (id_block[:, None] == id_block[None, :])
    attend = jnp.einsum("thd,shd->hts", query_block, key_block, preferred_element_type=jnp.float32)
    attend = jnp.where(allowed[None], attend, 0.0).astype(jnp.bfloat16)
    pulled = jnp.einsum("the,she->hts", grad_block, value_block, preferred_element_type=jnp.float32)
    pulled = jnp.where(allowed[None], pulled, 0.0).astype(jnp.bfloat16)
    output_part = jnp.einsum(
        "hts,she->the", attend, value_block, preferred_element_type=jnp.float32
    )
    query_part = jnp.einsum("hts,shd->thd", pulled, key_block, preferred_element_type=jnp.float32)
    key_part = jnp.einsum("hts,thd->shd", pulled, query_block, preferred_element_type=jnp.float32)
    value_part = jnp.einsum("hts,the->she", attend, grad_block, preferred_element_type=jnp.float32)
    return (output_part, query_part, key_part, value_part)


def local(queries, keys, values, out_weight, grad_out, doc_ids):
    row_count = queries.shape[0]
    local_heads = queries.shape[1] // HD
    ctx_count = lax.axis_size("ctx")
    total_rows = row_count * ctx_count
    factor = 1.0 / math.sqrt(HD * total_rows / DOCS)
    block_rows = min(512, row_count)
    block_count = row_count // block_rows
    full_grad = lax.all_gather(grad_out, "head", axis=1, tiled=True)
    grad_heads = lax.dot_general(
        full_grad, out_weight, (((1,), (1,)), ((), ())), preferred_element_type=jnp.float32
    ).astype(jnp.bfloat16)
    query_rows = queries.reshape(row_count, local_heads, HD)
    key_rows = keys.reshape(row_count, local_heads, HD)
    value_rows = values.reshape(row_count, local_heads, HD)
    grad_rows = grad_heads.reshape(row_count, local_heads, HD)
    query_blocks = query_rows.reshape(block_count, block_rows, local_heads, HD)
    key_blocks = key_rows.reshape(block_count, block_rows, local_heads, HD)
    value_blocks = value_rows.reshape(block_count, block_rows, local_heads, HD)
    grad_blocks = grad_rows.reshape(block_count, block_rows, local_heads, HD)
    id_blocks = doc_ids.reshape(block_count, block_rows)
    zero_state = jnp.zeros((local_heads, HD, HD), jnp.float32)
    no_mark = jnp.full((), -1, jnp.int32)

    def forward_turn(carried, pieces):
        key_block, value_block, id_block = pieces
        at_tail = (id_block == id_block[-1]).astype(jnp.bfloat16)[:, None, None]
        element = (
            jnp.einsum(
                "thd,the->hde", key_block * at_tail, value_block, preferred_element_type=jnp.float32
            ),
            id_block[-1],
        )
        return (chain_link(carried, element), carried)

    (key_summary, last_id), (prior_keys, prior_marks) = lax.scan(
        forward_turn, (zero_state, no_mark), (key_blocks, value_blocks, id_blocks)
    )

    def reverse_turn(carried, pieces):
        query_block, grad_block, id_block = pieces
        at_head = (id_block == id_block[0]).astype(jnp.bfloat16)[:, None, None]
        element = (
            jnp.einsum(
                "thd,the->hde",
                query_block * at_head,
                grad_block,
                preferred_element_type=jnp.float32,
            ),
            id_block[0],
        )
        return (chain_link(carried, element), carried)

    (query_summary, first_id), (later_queries, later_marks) = lax.scan(
        reverse_turn, (zero_state, no_mark), (query_blocks, grad_blocks, id_blocks), reverse=True
    )
    key_income, key_mark = prefix(
        (key_summary[None], last_id), "ctx", chain_link, (zero_state[None], no_mark), False
    )
    query_income, query_mark = prefix(
        (query_summary[None], first_id), "ctx", chain_link, (zero_state[None], no_mark), True
    )
    key_state = key_income[0]
    query_state = query_income[0]
    output_intra, query_intra, key_intra, value_intra = lax.map(
        block_terms, (query_blocks, key_blocks, value_blocks, grad_blocks, id_blocks)
    )
    near_keys = (id_blocks == prior_marks[:, None])[:, :, None, None]
    output_local = jnp.where(
        near_keys, exact_product("bthd,bhde->bthe", query_blocks, prior_keys), 0.0
    )
    query_local = jnp.where(
        near_keys, exact_product("bhde,bthe->bthd", prior_keys, grad_blocks), 0.0
    )
    near_queries = (id_blocks == later_marks[:, None])[:, :, None, None]
    key_local = jnp.where(
        near_queries, exact_product("bhde,bshe->bshd", later_queries, value_blocks), 0.0
    )
    value_local = jnp.where(
        near_queries, exact_product("bshd,bhde->bshe", key_blocks, later_queries), 0.0
    )
    from_before = (doc_ids == key_mark)[:, None, None]
    from_after = (doc_ids == query_mark)[:, None, None]
    output_income = jnp.where(
        from_before, exact_product("thd,hde->the", query_rows, key_state), 0.0
    )
    query_income_part = jnp.where(
        from_before, exact_product("hde,the->thd", key_state, grad_rows), 0.0
    )
    key_income_part = jnp.where(
        from_after, exact_product("hde,she->shd", query_state, value_rows), 0.0
    )
    value_income_part = jnp.where(
        from_after, exact_product("shd,hde->she", key_rows, query_state), 0.0
    )
    shape_rows = (row_count, local_heads, HD)
    attn_out = ((output_intra + output_local).reshape(shape_rows) + output_income) * factor
    attn_out = attn_out.astype(jnp.bfloat16)
    grad_queries = ((query_intra + query_local).reshape(shape_rows) + query_income_part) * factor
    grad_keys = ((key_intra + key_local).reshape(shape_rows) + key_income_part) * factor
    grad_values = ((value_intra + value_local).reshape(shape_rows) + value_income_part) * factor
    weight_factor = 1.0 / math.sqrt(total_rows)
    grad_weight = lax.psum_scatter(
        jnp.einsum("tj,the->jhe", full_grad, attn_out, preferred_element_type=jnp.float32)
        * weight_factor,
        "ctx",
        scatter_dimension=0,
        tiled=True,
    )
    flat_width = local_heads * HD
    return (
        grad_queries.astype(jnp.bfloat16).reshape(row_count, flat_width),
        grad_keys.astype(jnp.bfloat16).reshape(row_count, flat_width),
        grad_values.astype(jnp.bfloat16).reshape(row_count, flat_width),
        grad_weight,
    )


def solution(mesh):
    return jax.shard_map(
        local,
        mesh=mesh,
        in_specs=(
            P("ctx", "head"),
            P("ctx", "head"),
            P("ctx", "head"),
            P("head", None),
            P("ctx", "head"),
            P("ctx"),
        ),
        out_specs=(P("ctx", "head"), P("ctx", "head"), P("ctx", "head"), P("ctx", "head", None)),
        check_vma=False,
    )
```

profile of v0, /device:TPU:0, one launch (start us, length us, event | category | flops | bytes accessed | tf_op | source)
XLA Modules:
  0.0 859.0 jit_solution(137322698075764365)
XLA Ops:
  8.0 1.2 copy.73
  9.2 1.4 fusion.64
  10.6 2.0 compare_convert_fusion
  13.7 1.1 copy.76
  15.2 8.7 %all-gather.6.cloned.1.call-done = bf16[256,2048]{1,0:T(8,128)(2,1)} async-done(((bf16[256,1024]{1,0:T(8,128)(2,1)}), bf16[256,2048]{1,0:T(8,128)(2,1)}) %all-gather.6.cloned.1.call-update) | async-done | bytes 1048592 | tf_op jit(solution)/shard_map/all_gather | solution.py:74
  23.9 3.8 convolution_convert_fusion
  33.8 23.9 %all-reduce.2 = (s32[64]{0:T(128)S(1)}, s32[64]{0:T(128)S(1)}) all-reduce(s32[64]{0:T(128)S(1)} %dynamic-update-slice, s32[64]{0:T(128)S(1)} %dynamic-update-slice.1), channel_id=1, replica_groups=mesh['ctx'=64,'head'=2] {'ctx'}, use_global_device_ids=true, to_apply=%add | all-reduce | flops 128 | bytes 1024
  57.9 1.4 select_convert_fusion
  59.3 73.8 %all-gather.8.cloned.1.call-done = bf16[512,128,128]{2,1,0:T(8,128)(2,1)} async-done(((bf16[8,128,128]{2,1,0:T(8,128)(2,1)}), bf16[512,128,128]{2,1,0:T(8,128)(2,1)}) %all-gather.8.cloned.1.call-update) | async-done | bytes 16777232 | tf_op jit(solution)/shard_map/all_gather | solution.py:17
  133.2 107.4 %all-gather.10.cloned.1.call-done = bf16[512,128,128]{2,1,0:T(8,128)(2,1)} async-done(((bf16[8,128,128]{2,1,0:T(8,128)(2,1)}), bf16[512,128,128]{2,1,0:T(8,128)(2,1)}) %all-gather.10.cloned.1.call-update) | async-done | bytes 16777232 | tf_op jit(solution)/shard_map/all_gather | solution.py:17
  240.6 232.1 %while.7 = (s32[]{:T(128)}, f32[1,8,128,128]{3,2,1,0:T(8,128)S(1)}, s32[]{:T(128)}, s32[]{:T(128)}, bf16[64,1,8,128,128]{4,3,2,1,0:T(8,128)(2,1)}, /*index=5*/s3...) while((s32[]{:T(128)}, f32[1,8,128,128]{3,2,1,0:T(8,128)S(1)}, s32[]{:T(128)}, s32[]{:T(128)}, ...), condition=%wide.region_3.4_spmd, body=%wide.region_2.3_spmd.sunk | while | flops 393226 | bytes 1310918 | solution.py:32
  242.5 1.1 convert_add_fusion.5
  246.2 1.1 convert_add_fusion.5
  249.9 1.1 convert_add_fusion.5
  253.6 1.1 convert_add_fusion.5
  257.3 1.1 convert_add_fusion.5
  260.9 1.1 convert_add_fusion.5
  264.6 1.1 convert_add_fusion.5
  268.3 1.1 convert_add_fusion.5
  272.0 1.1 convert_add_fusion.5
  275.7 1.1 convert_add_fusion.5
  279.4 1.1 convert_add_fusion.5
  283.0 1.1 convert_add_fusion.5
  286.7 1.1 convert_add_fusion.5
  290.4 1.1 convert_add_fusion.5
  294.1 1.1 convert_add_fusion.5
  297.8 1.1 convert_add_fusion.5
  301.4 1.1 convert_add_fusion.5
  305.1 1.1 convert_add_fusion.5
  308.8 1.1 convert_add_fusion.5
  312.5 1.1 convert_add_fusion.5
  330.9 1.1 convert_add_fusion.5
  334.6 1.1 convert_add_fusion.5
  338.3 1.1 convert_add_fusion.5
  400.8 1.1 convert_add_fusion.5
  404.5 1.1 convert_add_fusion.5
  408.2 1.1 convert_add_fusion.5
  470.8 1.1 convert_add_fusion.5
  472.8 1.7 fusion.29
  474.5 1.7 fusion.15
  476.9 4.5 multiply_bitcast_fusion
  481.4 9.3 %copy.64 = f32[2048,8,128]{2,1,0:T(8,128)} copy(f32[2048,8,128]{0,2,1:T(8,128)} %multiply_bitcast_fusion) | data formatting | bytes 16777216 | tf_op jit(solution)/shard_map/mul | solution.py:169
  490.8 1.5 select_convert_fusion.1
  493.2 1.5 fusion.21
  494.7 2.0 copy.67
  497.3 1.5 fusion.19
  501.0 1.7 fusion.13
  504.4 348.0 %reduce-scatter.2.cloned.1.call-done = f32[32,8,128]{2,1,0:T(8,128)} async-done(((f32[2048,8,128]{2,1,0:T(8,128)}), f32[32,8,128]{2,1,0:T(8,128)}) %reduce-scatter.2.cloned.1.call-update) | async-done | bytes 131088 | tf_op jit(solution)/shard_map/reduce_scatter | solution.py:168
  (142 shorter events, 89.0 us)
Async XLA Ops:
  7.2 5.4 copy-start
  7.2 16.7 %all-gather.6.cloned.1.call-start = ((), (), s32[]{:S(2)}) async-start(), calls=%async_computation.1 | async-start | bytes 1572864 | tf_op jit(solution)/shard_map/all_gather | solution.py:74
  7.9 125.2 %all-gather.8.cloned.1.call-start = ((), (), s32[]{:S(2)}) async-start(), calls=%async_computation.3 | async-start | bytes 17039360 | tf_op jit(solution)/shard_map/all_gather | solution.py:17
  13.6 227.0 %all-gather.10.cloned.1.call-start = ((), (), s32[]{:S(2)}) async-start(), calls=%async_computation.4 | async-start | bytes 17039360 | tf_op jit(solution)/shard_map/all_gather | solution.py:17
  15.1 16.4 %copy-start.5 = (u32[128]{0:T(128)S(1)}, u32[128]{0:T(128)}, u32[]{:S(2)}) copy-start(u32[128]{0:T(128)} %constant.115) | copy-start | bytes 1540
  15.2 42.6 %copy-start.4 = (s32[256]{0:T(256)S(1)}, s32[256]{0:T(256)}, u32[]{:S(2)}) copy-start(s32[256]{0:T(256)} %param.15) | copy-start | bytes 3076
  15.2 42.7 %copy-start.2 = (bf16[256,1024]{1,0:T(8,128)(2,1)S(1)}, bf16[256,1024]{1,0:T(8,128)(2,1)}, u32[]{:S(2)}) copy-start(bf16[256,1024]{1,0:T(8,128)(2,1)} %param.10) | copy-start | bytes 1572868
  28.9 823.5 %reduce-scatter.2.cloned.1.call-start = ((), (), s32[]{:S(2)}) async-start(), calls=%async_computation.2 | async-start | bytes 8519680 | tf_op jit(solution)/shard_map/reduce_scatter | solution.py:168
  472.8 4.1 copy-start.3
  490.8 2.1 copy-start.1
Sparse Core Ops, SparseCore 0:
  9.7 14.1 all-gather.5
  27.3 105.7 all-gather.7
  136.6 103.9 all-gather.9
  490.9 361.5 reduce-scatter.1
where the time goes:
time: 872 us; the launch traced here: 859 us
  waiting for transfers between devices  539 us (62%)
  loops' own time  125 us (14%)
  other arithmetic  72.4 us (8%)
  local copies, waits for them, and re-layouts  57 us (7%)
  matrix products  25.3 us (3%)
  blocking collectives  23.9 us (3%)
  between operations  16.6 us (2%)
    reduce_scatter x1, waiting for transfers between devices, local(): lax.psum_scatter(jnp.einsum('tj,the->jhe', full_grad, attn_out, preferred...  348 us
    all_gather x2, waiting for transfers between devices, prefix(): lax.all_gather(a.astype(kind), axis)  181 us
    another operation x2, loops' own time, prefix(): return lax.fori_loop(0, ahead, one, state)  125 us
    add x63, other arithmetic, chain_link(): later_states + jnp.where(joined, earlier_states, jnp.zeros_like(earlier_s...  70.3 us
    dynamic_slice x63, local copies, waits for them, and re-layouts, one(): lax.dynamic_index_in_dim(a, source, 0, False).astype(own.dtype)  36.9 us
    unnamed x1, blocking collectives  23.9 us
  transfers between devices with their start and end apart: 4, of which 4 were waited for; matrix products, arithmetic and copies ran while one was open for 3% of the time, Pallas kernels for 0%

commit v1 on v0

v1 whole, which is shorter than its diff:
```python
import math

import jax
import jax.numpy as jnp
from jax import lax
from jax.experimental import pallas as pl
from jax.experimental.pallas import tpu as pltpu
from jax.sharding import PartitionSpec as P

HD = 128
DOCS = 4
SIDE = 4
PLANE = SIDE * SIDE
ROWS = 256
HEADS = 8
WIDTH = HEADS * HD
MODEL = 2 * WIDTH
PIECE = 64
BLOCK = 32
MESH = pl.DeviceIdType.MESH
COLOURS = (((0, 384), 0, 1, 2), ((384, 768), 1, 2, 0), ((768, 1024), 2, 0, 1))
F32 = jnp.float32
BF16 = jnp.bfloat16


def dot(a, b, dims=((1,), (0,))):
    return lax.dot_general(a, b, (dims, ((), ())), preferred_element_type=F32)


NT = ((1,), (1,))
TN = ((0,), (0,))


def kernel(
    factor, weight_factor,
    ids_ref, q_hbm, k_hbm, v_hbm, w_hbm, g_hbm,
    dq_hbm, dk_hbm, dv_hbm, gw_hbm,
    q_v, k_v, v_v, w_v, g_v, gh_v, gt_v,
    idc_v, allow_v, att_v, pul_v, o_v, dq_v, dk_v, dv_v, gw_v,
    ks_v, kr_v, kt_v, kz_v, kp_v, kb_v, s_v,
    qs_v, qr_v, qt_v, qz_v, qp_v, qb_v, t_v,
    gb_v, ab_v, s2_v, r2_v, s3_v, r3_v,
    loc, gx_s, gx_r,
    k1s, k1r, k2s, k2r, k3s, k3r,
    q1s, q1r, q2s, q2r, q3s, q3r,
    gs, gr, fs, fr, as_, ar, b2s, b2r, b3s, b3r,
):
    ctx = lax.axis_index("ctx")
    half = lax.axis_index("head")
    z = ctx // PLANE
    x = (ctx // SIDE) % SIDE
    y = ctx % SIDE
    me = ctx % PLANE
    pos = (z, x, y)

    def plane_peer(k):
        return ((z * PLANE + (me + k) % PLANE), half)

    def axis_peer(axis, d):
        p = [z, x, y]
        p[axis] = (p[axis] + d) % SIDE
        return (p[0] * PLANE + p[1] * SIDE + p[2], half)

    partner = (ctx, 1 - half)

    def remote(src, dst, ssem, rsem, peer):
        return pltpu.make_async_remote_copy(
            src_ref=src, dst_ref=dst, send_sem=ssem, recv_sem=rsem,
            device_id=peer, device_id_type=MESH,
        )

    load_k = pltpu.make_async_copy(k_hbm, k_v, loc.at[0])
    load_v = pltpu.make_async_copy(v_hbm, v_v, loc.at[1])
    load_g = pltpu.make_async_copy(g_hbm, g_v.at[half], loc.at[2])
    load_q = pltpu.make_async_copy(q_hbm, q_v, loc.at[3])
    load_w = pltpu.make_async_copy(w_hbm, w_v, loc.at[4])
    for load in (load_k, load_v, load_g, load_q, load_w):
        load.start()

    barrier = pltpu.get_barrier_semaphore()

    def greet(k, carry):
        pl.semaphore_signal(barrier, inc=1, device_id=plane_peer(k), device_id_type=MESH)
        return carry

    lax.fori_loop(1, PLANE, greet, 0)
    for d in (1, 2, 3):
        pl.semaphore_signal(barrier, inc=1, device_id=axis_peer(0, d), device_id_type=MESH)
    pl.semaphore_signal(barrier, inc=1, device_id=partner, device_id_type=MESH)

    id_row = ids_ref[...].astype(F32)
    id_col = jnp.transpose(jnp.broadcast_to(id_row, (HD, ROWS)))
    idc_v[...] = id_col
    first = id_col[0:1, :]
    last = id_col[ROWS - 1:ROWS, :]
    below = lax.broadcasted_iota(jnp.int32, (ROWS, ROWS), 0) >= lax.broadcasted_iota(
        jnp.int32, (ROWS, ROWS), 1
    )
    same = jnp.concatenate([id_col, id_col], axis=1) == id_row
    allow_v[...] = jnp.where(below & same, 1.0, 0.0).astype(F32)
    marks = jnp.concatenate(
        [jnp.broadcast_to(first, (8, HD)), jnp.broadcast_to(last, (8, HD))], axis=0
    ).astype(BF16)

    def cols(h):
        return pl.ds(pl.multiple_of(h * HD, HD), HD)

    def summarise(a_v, b_v, out_v, edge):
        mask = jnp.where(idc_v[...] == edge, 1.0, 0.0).astype(BF16)

        def one(h, carry):
            state = dot(a_v[:, cols(h)] * mask, b_v[:, cols(h)], TN).astype(BF16)
            out_v[2 * h, 0:PIECE, :] = state[0:PIECE]
            out_v[2 * h + 1, 0:PIECE, :] = state[PIECE:]
            out_v[2 * h, PIECE:, :] = marks
            out_v[2 * h + 1, PIECE:, :] = marks
            return carry

        lax.fori_loop(0, HEADS, one, 0)

    def plane_copies(src, dst, ssem, rsem):
        def make(k):
            return remote(
                src.at[(me + k) % PLANE], dst.at[me], ssem.at[k], rsem.at[k], plane_peer(k)
            )
        return make

    def start_all(make, count):
        def one(k, carry):
            make(k).start()
            return carry
        lax.fori_loop(1, count, one, 0)

    def recv_all(make, count):
        def one(k, carry):
            make(k).wait_recv()
            return carry
        lax.fori_loop(1, count, one, 0)

    def sent_all(make, count):
        def one(k, carry):
            make(k).wait_send()
            return carry
        lax.fori_loop(1, count, one, 0)

    def z_copies(src, dst, ssem, rsem):
        def make(d):
            return remote(src, dst.at[d], ssem.at[d], rsem.at[d], axis_peer(0, d))
        return make

    def scan_plane(recv, part, total, backward):
        order = range(PLANE - 1, -1, -1) if backward else range(PLANE)
        acc = jnp.zeros((PIECE, HD), F32)
        mark = None
        for m in order:
            ids = recv[m, PIECE:, :].astype(F32)
            first_m, last_m = ids[0:1], ids[8:9]
            near, far = (last_m, first_m) if backward else (first_m, last_m)
            item = recv[m, 0:PIECE, :].astype(F32)
            if mark is None:
                part[m] = jnp.zeros((PIECE, HD), F32)
                acc = item
            else:
                part[m] = acc * jnp.where(mark == near, 1.0, 0.0)
                acc = item + acc * jnp.where(mark == far, 1.0, 0.0)
            mark = far
        total[0:PIECE, :] = acc.astype(BF16)
        total[PIECE:, :] = jnp.broadcast_to(mark, (16, HD)).astype(BF16)

    def finish_prefix(recv, part, zrecv, back, backward):
        terms = []
        for d in (1, 2, 3):
            valid = (d > z) if backward else (d <= z)
            keep = jnp.where(valid, 1.0, 0.0)
            terms.append((zrecv[d, 0:PIECE, :].astype(F32) * keep, zrecv[d, PIECE:, :].astype(F32)[0:1]))

        def one(m, carry):
            ids = recv[m, PIECE:, :].astype(F32)
            near = ids[8:9] if backward else ids[0:1]
            value = part[m]
            for term, mark in terms:
                value = value + term * jnp.where(mark == near, 1.0, 0.0)
            back[m] = value.astype(BF16)
            return carry

        lax.fori_loop(0, PLANE, one, 0)

    load_k.wait()
    load_v.wait()
    summarise(k_v, v_v, ks_v, last)
    kr_v[me] = ks_v[me]
    load_g.wait()

    def flip(hf):
        def one(j, carry):
            zz = 2 * hf + j // SIDE
            xx = j % SIDE
            block = jnp.transpose(g_v[hf, :, cols(j)])
            gt_v[zz, xx] = block.reshape(SIDE, BLOCK, ROWS)
            return carry
        lax.fori_loop(0, HEADS, one, 0)

    flip(half)
    pl.semaphore_wait(barrier, PLANE - 1 + 3 + 1)

    give_g = remote(g_v.at[half], g_v.at[half], gx_s, gx_r, partner)
    give_g.start()
    k1 = plane_copies(ks_v, kr_v, k1s, k1r)
    start_all(k1, PLANE)

    def slice_of(colour, q):
        axis = COLOURS[colour][1]
        if axis == 0:
            return gt_v.at[q, pl.ds(2 * half, 2)]
        if axis == 1:
            return gt_v.at[pl.ds(2 * half, 2), q]
        return gt_v.at[pl.ds(2 * half, 2), :, q]

    def g_copy(colour, d):
        axis = COLOURS[colour][1]
        return remote(
            slice_of(colour, (pos[axis] + d) % SIDE),
            gb_v.at[colour, d, pl.ds(2 * half, 2)],
            gs.at[colour, d], gr.at[colour, d], axis_peer(axis, d),
        )

    def g_pass(colour, d):
        part = gb_v.at[colour, d, pl.ds(2 * half, 2)]
        return remote(part, part, fs.at[colour, d], fr.at[colour, d], partner)

    for colour in (1, 2):
        for d in (1, 3, 2):
            g_copy(colour, d).start()

    load_q.wait()

    def attend_head(h, carry):
        a = dot(q_v[:, cols(h)], k_v[:, cols(h)], NT) * allow_v[...]
        a = a.astype(BF16)
        att_v[h] = a
        o_v[:, cols(h)] = dot(a, v_v[:, cols(h)])
        return carry

    lax.fori_loop(0, HEADS, attend_head, 0)

    give_g.wait_recv()
    load_w.wait()

    def grad_chunk(c, carry):
        rows = pl.ds(pl.multiple_of(c * 256, 256), 256)
        value = dot(g_v[0], w_v[rows, 0:WIDTH], NT) + dot(g_v[1], w_v[rows, WIDTH:], NT)
        gh_v[:, rows] = value.astype(BF16)
        return carry

    lax.fori_loop(0, WIDTH // 256, grad_chunk, 0)
    summarise(q_v, gh_v, qs_v, first)
    qr_v[me] = qs_v[me]

    recv_all(k1, PLANE)
    scan_plane(kr_v, kp_v, kt_v, False)
    k2 = z_copies(kt_v, kz_v, k2s, k2r)
    start_all(k2, SIDE)
    q1 = plane_copies(qs_v, qr_v, q1s, q1r)
    start_all(q1, PLANE)

    flip(1 - half)
    for d in (1, 3, 2):
        g_copy(0, d).start()
    for colour in range(3):
        axis = COLOURS[colour][1]
        q = pos[axis]
        if axis == 0:
            gb_v[colour, 0] = gt_v[q]
        elif axis == 1:
            gb_v[colour, 0] = gt_v[:, q]
        else:
            gb_v[colour, 0] = gt_v[:, :, q]

    recv_all(k2, SIDE)
    finish_prefix(kr_v, kp_v, kz_v, kb_v, False)
    k3 = plane_copies(kb_v, s_v, k3s, k3r)
    start_all(k3, PLANE)
    s_v[me] = kb_v[me]

    def pulled_head(h, carry):
        p = dot(gh_v[:, cols(h)], v_v[:, cols(h)], NT) * allow_v[...]
        p = p.astype(BF16)
        dq_v[:, cols(h)] = dot(p, k_v[:, cols(h)])
        dk_v[:, cols(h)] = dot(p, q_v[:, cols(h)], TN)
        dv_v[:, cols(h)] = dot(att_v[h], gh_v[:, cols(h)], TN)
        return carry

    lax.fori_loop(0, HEADS, pulled_head, 0)

    recv_all(q1, PLANE)
    scan_plane(qr_v, qp_v, qt_v, True)
    q2 = z_copies(qt_v, qz_v, q2s, q2r)
    start_all(q2, SIDE)

    recv_all(k3, PLANE)

    def out_head(h, carry):
        keep = jnp.where(idc_v[...] == idc_v[0:1, :], factor, 0.0)
        state = s_v[pl.ds(2 * h, 2)].reshape(HD, HD)
        o = o_v[:, cols(h)] * factor + dot(q_v[:, cols(h)], state) * keep
        ab_v[0, :, cols(h)] = o.astype(BF16)
        return carry

    def a_copy(colour, d):
        (lo, hi), axis = COLOURS[colour][:2]
        return remote(
            ab_v.at[0, :, lo:hi], ab_v.at[d, :, lo:hi],
            as_.at[colour, d], ar.at[colour, d], axis_peer(axis, d),
        )

    for colour in range(3):
        lo, hi = COLOURS[colour][0]
        lax.fori_loop(lo // HD, hi // HD, out_head, 0)
        for d in (1, 3, 2):
            a_copy(colour, d).start()

    recv_all(q2, SIDE)
    finish_prefix(qr_v, qp_v, qz_v, qb_v, True)
    q3 = plane_copies(qb_v, t_v, q3s, q3r)
    start_all(q3, PLANE)
    t_v[me] = qb_v[me]

    for colour in (1, 2, 0):
        for d in (1, 3, 2):
            g_copy(colour, d).wait_recv()
            g_pass(colour, d).start()

    def dq_head(h, carry):
        keep = jnp.where(idc_v[...] == idc_v[0:1, :], factor, 0.0)
        state = s_v[pl.ds(2 * h, 2)].reshape(HD, HD)
        dq = dq_v[:, cols(h)] * factor + dot(gh_v[:, cols(h)], state, NT) * keep
        q_v[:, cols(h)] = dq.astype(BF16)
        return carry

    lax.fori_loop(0, HEADS, dq_head, 0)
    put_q = pltpu.make_async_copy(q_v, dq_hbm, loc.at[5])
    put_q.start()

    def s2_copy(colour, d):
        (lo, hi), _, axis, _ = COLOURS[colour]
        return remote(
            s2_v.at[(pos[axis] + d) % SIDE, :, lo:hi], r2_v.at[d, :, lo:hi],
            b2s.at[colour, d], b2r.at[colour, d], axis_peer(axis, d),
        )

    def s3_copy(colour, d):
        (lo, hi), _, _, axis = COLOURS[colour]
        return remote(
            s3_v.at[(pos[axis] + d) % SIDE, :, lo:hi], r3_v.at[d, :, lo:hi],
            b3s.at[colour, d], b3r.at[colour, d], axis_peer(axis, d),
        )

    for colour in range(3):
        (lo, hi), _, axis, _ = COLOURS[colour]
        for d in (1, 3, 2):
            g_pass(colour, d).wait_recv()
        for d in (1, 3, 2):
            a_copy(colour, d).wait_recv()

        def product(o, carry):
            value = dot(gb_v[colour, 0, o].reshape(128, ROWS), ab_v[0, :, lo:hi])
            for d in (1, 2, 3):
                value = value + dot(gb_v[colour, d, o].reshape(128, ROWS), ab_v[d, :, lo:hi])
            value = value.astype(BF16)
            if axis == 2:
                for i in range(SIDE):
                    s2_v[i, pl.ds(pl.multiple_of(o * BLOCK, BLOCK), BLOCK), lo:hi] = value[
                        i * BLOCK:(i + 1) * BLOCK
                    ]
            else:
                s2_v[o, :, lo:hi] = value
            return carry

        lax.fori_loop(0, SIDE, product, 0)
        for d in (1, 3, 2):
            s2_copy(colour, d).start()

    recv_all(q3, PLANE)

    def kv_head(h, carry):
        keep = jnp.where(idc_v[...] == idc_v[ROWS - 1:ROWS, :], factor, 0.0)
        state = t_v[pl.ds(2 * h, 2)].reshape(HD, HD)
        vh = v_v[:, cols(h)]
        kh = k_v[:, cols(h)]
        dk = dk_v[:, cols(h)] * factor + dot(vh, state, NT) * keep
        dv = dv_v[:, cols(h)] * factor + dot(kh, state) * keep
        k_v[:, cols(h)] = dk.astype(BF16)
        v_v[:, cols(h)] = dv.astype(BF16)
        return carry

    lax.fori_loop(0, HEADS, kv_head, 0)
    put_k = pltpu.make_async_copy(k_v, dk_hbm, loc.at[6])
    put_v = pltpu.make_async_copy(v_v, dv_hbm, loc.at[7])
    put_k.start()
    put_v.start()

    for colour in range(3):
        (lo, hi), _, axis, _ = COLOURS[colour]
        for d in (1, 3, 2):
            s2_copy(colour, d).wait_recv()
        for i in range(SIDE):
            rows = slice(i * BLOCK, (i + 1) * BLOCK)
            value = s2_v[pos[axis], rows, lo:hi].astype(F32)
            for d in (1, 2, 3):
                value = value + r2_v[d, rows, lo:hi].astype(F32)
            s3_v[i, :, lo:hi] = value.astype(BF16)
        for d in (1, 3, 2):
            s3_copy(colour, d).start()

    for colour in range(3):
        (lo, hi), _, _, axis = COLOURS[colour]
        for d in (1, 3, 2):
            s3_copy(colour, d).wait_recv()
        value = s3_v[pos[axis], :, lo:hi].astype(F32)
        for d in (1, 2, 3):
            value = value + r3_v[d, :, lo:hi].astype(F32)
        value = value * weight_factor
        for h in range(lo // HD, hi // HD):
            gw_v[:, h, :] = value[:, h * HD - lo:(h + 1) * HD - lo]
    put_w = pltpu.make_async_copy(gw_v, gw_hbm, loc.at[8])
    put_w.start()

    give_g.wait_send()
    for make in (k1, q1, k3, q3):
        sent_all(make, PLANE)
    for make in (k2, q2):
        sent_all(make, SIDE)
    for colour in range(3):
        for d in (1, 2, 3):
            g_copy(colour, d).wait_send()
            g_pass(colour, d).wait_send()
            a_copy(colour, d).wait_send()
            s2_copy(colour, d).wait_send()
            s3_copy(colour, d).wait_send()
    for put in (put_q, put_k, put_v, put_w):
        put.wait()


def local(queries, keys, values, out_weight, grad_out, doc_ids):
    total_rows = ROWS * lax.axis_size("ctx")
    factor = 1.0 / math.sqrt(HD * total_rows / DOCS)
    weight_factor = 1.0 / math.sqrt(total_rows)
    dma = pltpu.SemaphoreType.DMA

    def vm(*shape, dtype=BF16):
        return pltpu.VMEM(shape, dtype)

    prefix = [
        vm(PLANE, PIECE + 16, HD), vm(PLANE, PIECE + 16, HD), vm(PIECE + 16, HD),
        vm(SIDE, PIECE + 16, HD), vm(PLANE, PIECE, HD, dtype=F32), vm(PLANE, PIECE, HD),
        vm(PLANE, PIECE, HD),
    ]
    prefix_sems = [dma((PLANE,)), dma((PLANE,)), dma((SIDE,)), dma((SIDE,)), dma((PLANE,)), dma((PLANE,))]
    flat = (ROWS, WIDTH)
    scratch = [
        vm(*flat), vm(*flat), vm(*flat), vm(WIDTH, MODEL), vm(2, *flat), vm(*flat),
        vm(SIDE, SIDE, SIDE, BLOCK, ROWS),
        vm(ROWS, HD, dtype=F32), vm(ROWS, ROWS, dtype=F32), vm(HEADS, ROWS, ROWS),
        vm(8, 128), vm(*flat, dtype=F32), vm(*flat, dtype=F32), vm(*flat, dtype=F32),
        vm(*flat, dtype=F32), vm(BLOCK, HEADS, HD, dtype=F32),
        *prefix, *prefix,
        vm(3, SIDE, SIDE, SIDE, BLOCK, ROWS), vm(SIDE, *flat),
        vm(SIDE, 128, WIDTH), vm(SIDE, 128, WIDTH), vm(SIDE, BLOCK, WIDTH), vm(SIDE, BLOCK, WIDTH),
        dma((9,)), dma(()), dma(()),
        *prefix_sems, *prefix_sems,
        *[dma((3, SIDE)) for _ in range(10)],
    ]
    any_space = pl.BlockSpec(memory_space=pl.ANY)
    shape = jax.ShapeDtypeStruct
    return pl.pallas_call(
        lambda *refs: kernel(factor, weight_factor, *refs),
        out_shape=(
            shape(flat, BF16), shape(flat, BF16), shape(flat, BF16),
            shape((BLOCK, HEADS, HD), F32),
        ),
        in_specs=[pl.BlockSpec(memory_space=pltpu.VMEM)] + [any_space] * 5,
        out_specs=(any_space,) * 4,
        scratch_shapes=scratch,
        compiler_params=pltpu.CompilerParams(collective_id=0, has_side_effects=True),
        name="linear_attention_backward",
    )(doc_ids.reshape(1, ROWS), queries, keys, values, out_weight, grad_out)


def solution(mesh):
    return jax.shard_map(
        local,
        mesh=mesh,
        in_specs=(
            P("ctx", "head"),
            P("ctx", "head"),
            P("ctx", "head"),
            P("head", None),
            P("ctx", "head"),
            P("ctx"),
        ),
        out_specs=(P("ctx", "head"), P("ctx", "head"), P("ctx", "head"), P("ctx", "head", None)),
        check_vma=False,
    )
```

time: 872 us -> 63.4 us (0.07); the launches traced: 859 us -> 63.1 us
  waiting for transfers between devices: 539 us -> 0 us
  loops' own time: 125 us -> 0 us
  other arithmetic: 72.4 us -> 0 us
  Pallas kernels: 0 us -> 55.3 us
  local copies, waits for them, and re-layouts: 57 us -> 7.17 us
  matrix products: 25.3 us -> 0 us
  blocking collectives: 23.9 us -> 0 us
  between operations: 16.6 us -> 0.64 us
    reduce_scatter x1 -> x0, waiting for transfers between devices: 348 us -> none  [local(): lax.psum_scatter(jnp.einsum('tj,the->jhe', full_grad, attn_out, preferred...]
    all_gather x3 -> x0, waiting for transfers between devices: 190 us -> none  [the longest x2 181 us: prefix(): lax.all_gather(a.astype(kind), axis)]
    another operation x2 -> x0, loops' own time: 125 us -> none  [prefix(): return lax.fori_loop(0, ahead, one, state)]
    add x63 -> x0, other arithmetic: 70.3 us -> none  [chain_link(): later_states + jnp.where(joined, earlier_states, jnp.zeros_like(earlier_s...]
    pallas_call x0 -> x1, Pallas kernels: none -> 55.3 us  [local(): pl.pallas_call(lambda *refs: kernel(factor, weight_factor, *refs), out_sh...]
    dynamic_slice x63 -> x0, local copies, waits for them, and re-layouts: 36.9 us -> none  [one(): lax.dynamic_index_in_dim(a, source, 0, False).astype(own.dtype)]
    dot_general x18 -> x0, matrix products: 25.3 us -> none  [the longest x8 6.81 us: exact_product(): jnp.einsum(form, left.astype(jnp.float32), right.astype(jnp.float32), pre...]
    unnamed x1 -> x0, blocking collectives: 23.9 us -> none
  transfers between devices with their start and end apart: 4 -> 0, of which waited for: 4 -> 0; matrix products, arithmetic and copies ran while one was open for 3% -> 0% of each run, Pallas kernels for 0% -> 0%
where the time goes in v1:
time: 63.4 us; the launch traced here: 63.1 us
  Pallas kernels  55.3 us (87%)
  local copies, waits for them, and re-layouts  7.17 us (11%)
  between operations  0.64 us (1%)
    pallas_call x1, Pallas kernels, local(): pl.pallas_call(lambda *refs: kernel(factor, weight_factor, *refs), out_sh...  55.3 us
    unnamed x4, local copies, waits for them, and re-layouts  7.17 us

profile of v1, /device:TPU:0, one launch (start us, length us, event | category | flops | bytes accessed | tf_op | source)
XLA Modules:
  0.0 63.1 jit_solution(5871563607547812384)
XLA Ops:
  0.6 55.3 %linear_attention_backward.1 = (bf16[256,1024]{1,0:T(8,128)(2,1)}, bf16[256,1024]{1,0:T(8,128)(2,1)}, bf16[256,1024]{1,0:T(8,128)(2,1)}, f32[32,8,128]{2,1,0:T(8,128)}) custom-call(s32[1,256]{1,0:T(1,128)} %bitcast.1, bf16[256,1024]{1,0:T(8,128)(2,1)} %refs_1_.1, bf16[256,1024]{1,0:T(8,128)(2,1)} %refs_2_.1, bf16[256,1024]{1,0:T(8,128)(2,1)} %refs_3_.1, ...), custom_call_target="tpu_custom_call" | custom-call | tf_op jit(solution)/shard_map/linear_attention_backward/pallas_call | solution.py:475
  55.9 1.9 %copy.14 = bf16[256,1024]{1,0:T(8,128)(2,1)} copy(bf16[256,1024]{1,0:T(8,128)(2,1)} %get-tuple-element.8) | data formatting | bytes 1048576
  57.8 1.9 %copy.15 = bf16[256,1024]{1,0:T(8,128)(2,1)} copy(bf16[256,1024]{1,0:T(8,128)(2,1)} %get-tuple-element.9) | data formatting | bytes 1048576
  59.6 1.9 %copy.16 = bf16[256,1024]{1,0:T(8,128)(2,1)} copy(bf16[256,1024]{1,0:T(8,128)(2,1)} %get-tuple-element.10) | data formatting | bytes 1048576
  61.5 1.6 %copy.17 = f32[32,8,128]{2,1,0:T(8,128)} copy(f32[32,8,128]{2,1,0:T(8,128)} %get-tuple-element.11) | data formatting | bytes 262144

commit v2 on v1

--- a/solution.py
+++ b/solution.py
@@ -36,7 +36,7 @@
     ids_ref, q_hbm, k_hbm, v_hbm, w_hbm, g_hbm,
     dq_hbm, dk_hbm, dv_hbm, gw_hbm,
     q_v, k_v, v_v, w_v, g_v, gh_v, gt_v,
-    idc_v, allow_v, att_v, pul_v, o_v, dq_v, dk_v, dv_v, gw_v,
+    idc_v, allow_v, att_v, o_v, dq_v, dk_v, dv_v, gw_v,
     ks_v, kr_v, kt_v, kz_v, kp_v, kb_v, s_v,
     qs_v, qr_v, qt_v, qz_v, qp_v, qb_v, t_v,
     gb_v, ab_v, s2_v, r2_v, s3_v, r3_v,
@@ -116,7 +116,7 @@
             out_v[2 * h + 1, PIECE:, :] = marks
             return carry
 
-        lax.fori_loop(0, HEADS, one, 0)
+        lax.fori_loop(0, HEADS, one, 0, unroll=True)
 
     def plane_copies(src, dst, ssem, rsem):
         def make(k):
@@ -183,13 +183,7 @@
             back[m] = value.astype(BF16)
             return carry
 
-        lax.fori_loop(0, PLANE, one, 0)
-
-    load_k.wait()
-    load_v.wait()
-    summarise(k_v, v_v, ks_v, last)
-    kr_v[me] = ks_v[me]
-    load_g.wait()
+        lax.fori_loop(0, PLANE, one, 0, unroll=True)
 
     def flip(hf):
         def one(j, carry):
@@ -198,41 +192,7 @@
             block = jnp.transpose(g_v[hf, :, cols(j)])
             gt_v[zz, xx] = block.reshape(SIDE, BLOCK, ROWS)
             return carry
-        lax.fori_loop(0, HEADS, one, 0)
-
-    flip(half)
-    pl.semaphore_wait(barrier, PLANE - 1 + 3 + 1)
-
-    give_g = remote(g_v.at[half], g_v.at[half], gx_s, gx_r, partner)
-    give_g.start()
-    k1 = plane_copies(ks_v, kr_v, k1s, k1r)
-    start_all(k1, PLANE)
-
-    def slice_of(colour, q):
-        axis = COLOURS[colour][1]
-        if axis == 0:
-            return gt_v.at[q, pl.ds(2 * half, 2)]
-        if axis == 1:
-            return gt_v.at[pl.ds(2 * half, 2), q]
-        return gt_v.at[pl.ds(2 * half, 2), :, q]
-
-    def g_copy(colour, d):
-        axis = COLOURS[colour][1]
-        return remote(
-            slice_of(colour, (pos[axis] + d) % SIDE),
-            gb_v.at[colour, d, pl.ds(2 * half, 2)],
-            gs.at[colour, d], gr.at[colour, d], axis_peer(axis, d),
-        )
-
-    def g_pass(colour, d):
-        part = gb_v.at[colour, d, pl.ds(2 * half, 2)]
-        return remote(part, part, fs.at[colour, d], fr.at[colour, d], partner)
-
-    for colour in (1, 2):
-        for d in (1, 3, 2):
-            g_copy(colour, d).start()
-
-    load_q.wait()
+        lax.fori_loop(0, HEADS, one, 0, unroll=True)
 
     def attend_head(h, carry):
         a = dot(q_v[:, cols(h)], k_v[:, cols(h)], NT) * allow_v[...]
@@ -241,46 +201,11 @@
         o_v[:, cols(h)] = dot(a, v_v[:, cols(h)])
         return carry
 
-    lax.fori_loop(0, HEADS, attend_head, 0)
-
-    give_g.wait_recv()
-    load_w.wait()
-
     def grad_chunk(c, carry):
         rows = pl.ds(pl.multiple_of(c * 256, 256), 256)
         value = dot(g_v[0], w_v[rows, 0:WIDTH], NT) + dot(g_v[1], w_v[rows, WIDTH:], NT)
         gh_v[:, rows] = value.astype(BF16)
         return carry
-
-    lax.fori_loop(0, WIDTH // 256, grad_chunk, 0)
-    summarise(q_v, gh_v, qs_v, first)
-    qr_v[me] = qs_v[me]
-
-    recv_all(k1, PLANE)
-    scan_plane(kr_v, kp_v, kt_v, False)
-    k2 = z_copies(kt_v, kz_v, k2s, k2r)
-    start_all(k2, SIDE)
-    q1 = plane_copies(qs_v, qr_v, q1s, q1r)
-    start_all(q1, PLANE)
-
-    flip(1 - half)
-    for d in (1, 3, 2):
-        g_copy(0, d).start()
-    for colour in range(3):
-        axis = COLOURS[colour][1]
-        q = pos[axis]
-        if axis == 0:
-            gb_v[colour, 0] = gt_v[q]
-        elif axis == 1:
-            gb_v[colour, 0] = gt_v[:, q]
-        else:
-            gb_v[colour, 0] = gt_v[:, :, q]
-
-    recv_all(k2, SIDE)
-    finish_prefix(kr_v, kp_v, kz_v, kb_v, False)
-    k3 = plane_copies(kb_v, s_v, k3s, k3r)
-    start_all(k3, PLANE)
-    s_v[me] = kb_v[me]
 
     def pulled_head(h, carry):
         p = dot(gh_v[:, cols(h)], v_v[:, cols(h)], NT) * allow_v[...]
@@ -290,15 +215,6 @@
         dv_v[:, cols(h)] = dot(att_v[h], gh_v[:, cols(h)], TN)
         return carry
 
-    lax.fori_loop(0, HEADS, pulled_head, 0)
-
-    recv_all(q1, PLANE)
-    scan_plane(qr_v, qp_v, qt_v, True)
-    q2 = z_copies(qt_v, qz_v, q2s, q2r)
-    start_all(q2, SIDE)
-
-    recv_all(k3, PLANE)
-
     def out_head(h, carry):
         keep = jnp.where(idc_v[...] == idc_v[0:1, :], factor, 0.0)
         state = s_v[pl.ds(2 * h, 2)].reshape(HD, HD)
@@ -306,81 +222,12 @@
         ab_v[0, :, cols(h)] = o.astype(BF16)
         return carry
 
-    def a_copy(colour, d):
-        (lo, hi), axis = COLOURS[colour][:2]
-        return remote(
-            ab_v.at[0, :, lo:hi], ab_v.at[d, :, lo:hi],
-            as_.at[colour, d], ar.at[colour, d], axis_peer(axis, d),
-        )
-
-    for colour in range(3):
-        lo, hi = COLOURS[colour][0]
-        lax.fori_loop(lo // HD, hi // HD, out_head, 0)
-        for d in (1, 3, 2):
-            a_copy(colour, d).start()
-
-    recv_all(q2, SIDE)
-    finish_prefix(qr_v, qp_v, qz_v, qb_v, True)
-    q3 = plane_copies(qb_v, t_v, q3s, q3r)
-    start_all(q3, PLANE)
-    t_v[me] = qb_v[me]
-
-    for colour in (1, 2, 0):
-        for d in (1, 3, 2):
-            g_copy(colour, d).wait_recv()
-            g_pass(colour, d).start()
-
     def dq_head(h, carry):
         keep = jnp.where(idc_v[...] == idc_v[0:1, :], factor, 0.0)
         state = s_v[pl.ds(2 * h, 2)].reshape(HD, HD)
         dq = dq_v[:, cols(h)] * factor + dot(gh_v[:, cols(h)], state, NT) * keep
         q_v[:, cols(h)] = dq.astype(BF16)
         return carry
-
-    lax.fori_loop(0, HEADS, dq_head, 0)
-    put_q = pltpu.make_async_copy(q_v, dq_hbm, loc.at[5])
-    put_q.start()
-
-    def s2_copy(colour, d):
-        (lo, hi), _, axis, _ = COLOURS[colour]
-        return remote(
-            s2_v.at[(pos[axis] + d) % SIDE, :, lo:hi], r2_v.at[d, :, lo:hi],
-            b2s.at[colour, d], b2r.at[colour, d], axis_peer(axis, d),
-        )
-
-    def s3_copy(colour, d):
-        (lo, hi), _, _, axis = COLOURS[colour]
-        return remote(
-            s3_v.at[(pos[axis] + d) % SIDE, :, lo:hi], r3_v.at[d, :, lo:hi],
-            b3s.at[colour, d], b3r.at[colour, d], axis_peer(axis, d),
-        )
-
-    for colour in range(3):
-        (lo, hi), _, axis, _ = COLOURS[colour]
-        for d in (1, 3, 2):
-            g_pass(colour, d).wait_recv()
-        for d in (1, 3, 2):
-            a_copy(colour, d).wait_recv()
-
-        def product(o, carry):
-            value = dot(gb_v[colour, 0, o].reshape(128, ROWS), ab_v[0, :, lo:hi])
-            for d in (1, 2, 3):
-                value = value + dot(gb_v[colour, d, o].reshape(128, ROWS), ab_v[d, :, lo:hi])
-            value = value.astype(BF16)
-            if axis == 2:
-                for i in range(SIDE):
-                    s2_v[i, pl.ds(pl.multiple_of(o * BLOCK, BLOCK), BLOCK), lo:hi] = value[
-                        i * BLOCK:(i + 1) * BLOCK
-                    ]
-            else:
-                s2_v[o, :, lo:hi] = value
-            return carry
-
-        lax.fori_loop(0, SIDE, product, 0)
-        for d in (1, 3, 2):
-            s2_copy(colour, d).start()
-
-    recv_all(q3, PLANE)
 
     def kv_head(h, carry):
         keep = jnp.where(idc_v[...] == idc_v[ROWS - 1:ROWS, :], factor, 0.0)
@@ -393,12 +240,141 @@
         v_v[:, cols(h)] = dv.astype(BF16)
         return carry
 
-    lax.fori_loop(0, HEADS, kv_head, 0)
-    put_k = pltpu.make_async_copy(k_v, dk_hbm, loc.at[6])
-    put_v = pltpu.make_async_copy(v_v, dv_hbm, loc.at[7])
-    put_k.start()
-    put_v.start()
-
+    give_g = remote(g_v.at[half], g_v.at[half], gx_s, gx_r, partner)
+    k1 = plane_copies(ks_v, kr_v, k1s, k1r)
+    k2 = z_copies(kt_v, kz_v, k2s, k2r)
+    k3 = plane_copies(kb_v, s_v, k3s, k3r)
+    q1 = plane_copies(qs_v, qr_v, q1s, q1r)
+    q2 = z_copies(qt_v, qz_v, q2s, q2r)
+    q3 = plane_copies(qb_v, t_v, q3s, q3r)
+
+    def slice_of(colour, q):
+        axis = COLOURS[colour][1]
+        if axis == 0:
+            return gt_v.at[q, pl.ds(2 * half, 2)]
+        if axis == 1:
+            return gt_v.at[pl.ds(2 * half, 2), q]
+        return gt_v.at[pl.ds(2 * half, 2), :, q]
+
+    def g_copy(colour, d):
+        axis = COLOURS[colour][1]
+        return remote(
+            slice_of(colour, (pos[axis] + d) % SIDE),
+            gb_v.at[colour, d, pl.ds(2 * half, 2)],
+            gs.at[colour, d], gr.at[colour, d], axis_peer(axis, d),
+        )
+
+    def g_pass(colour, d):
+        part = gb_v.at[colour, d, pl.ds(2 * half, 2)]
+        return remote(part, part, fs.at[colour, d], fr.at[colour, d], partner)
+
+    def a_copy(colour, d):
+        (lo, hi), axis = COLOURS[colour][:2]
+        return remote(
+            ab_v.at[0, :, lo:hi], ab_v.at[d, :, lo:hi],
+            as_.at[colour, d], ar.at[colour, d], axis_peer(axis, d),
+        )
+
+    def s2_copy(colour, d):
+        (lo, hi), _, axis, _ = COLOURS[colour]
+        return remote(
+            s2_v.at[(pos[axis] + d) % SIDE, :, lo:hi], r2_v.at[d, :, lo:hi],
+            b2s.at[colour, d], b2r.at[colour, d], axis_peer(axis, d),
+        )
+
+    def s3_copy(colour, d):
+        (lo, hi), _, _, axis = COLOURS[colour]
+        return remote(
+            s3_v.at[(pos[axis] + d) % SIDE, :, lo:hi], r3_v.at[d, :, lo:hi],
+            b3s.at[colour, d], b3r.at[colour, d], axis_peer(axis, d),
+        )
+
+    def product(colour):
+        (lo, hi), _, axis, _ = COLOURS[colour]
+        for d in (1, 3, 2):
+            g_pass(colour, d).wait_recv()
+        for d in (1, 3, 2):
+            a_copy(colour, d).wait_recv()
+        for o in range(SIDE):
+            value = dot(gb_v[colour, 0, o].reshape(128, ROWS), ab_v[0, :, lo:hi])
+            for d in (1, 2, 3):
+                value = value + dot(gb_v[colour, d, o].reshape(128, ROWS), ab_v[d, :, lo:hi])
+            value = value.astype(BF16)
+            if axis == 2:
+                for i in range(SIDE):
+                    s2_v[i, o * BLOCK:(o + 1) * BLOCK, lo:hi] = value[i * BLOCK:(i + 1) * BLOCK]
+            else:
+                s2_v[o, :, lo:hi] = value
+        for d in (1, 3, 2):
+            s2_copy(colour, d).start()
+
+    def own_slices():
+        gb_v[0, 0] = gt_v[z]
+        gb_v[1, 0] = gt_v[:, x]
+        gb_v[2, 0] = gt_v[:, :, y]
+
+    def pass_on(colour):
+        for d in (1, 3, 2):
+            g_copy(colour, d).wait_recv()
+            g_pass(colour, d).start()
+
+    def send_g(colour):
+        for d in (1, 3, 2):
+            g_copy(colour, d).start()
+
+    load_k.wait()
+    load_v.wait()
+    summarise(k_v, v_v, ks_v, last)
+    kr_v[me] = ks_v[me]
+    load_q.wait()
+    lax.fori_loop(0, HEADS, attend_head, 0, unroll=True)
+    load_g.wait()
+    flip(half)
+    pl.semaphore_wait(barrier, PLANE - 1 + 3 + 1)
+
+    start_all(k1, PLANE)
+    give_g.start()
+    send_g(1)
+    send_g(2)
+    give_g.wait_recv()
+    load_w.wait()
+    lax.fori_loop(0, WIDTH // 256, grad_chunk, 0, unroll=True)
+    summarise(q_v, gh_v, qs_v, first)
+    qr_v[me] = qs_v[me]
+    flip(1 - half)
+    recv_all(k1, PLANE)
+    scan_plane(kr_v, kp_v, kt_v, False)
+    start_all(k2, SIDE)
+    send_g(0)
+    own_slices()
+    recv_all(k2, SIDE)
+    finish_prefix(kr_v, kp_v, kz_v, kb_v, False)
+    start_all(k3, PLANE)
+    s_v[me] = kb_v[me]
+    start_all(q1, PLANE)
+    lax.fori_loop(0, HEADS, pulled_head, 0, unroll=True)
+
+    recv_all(k3, PLANE)
+    for colour in range(3):
+        lo, hi = COLOURS[colour][0]
+        lax.fori_loop(lo // HD, hi // HD, out_head, 0, unroll=True)
+        for d in (1, 3, 2):
+            a_copy(colour, d).start()
+    recv_all(q1, PLANE)
+    scan_plane(qr_v, qp_v, qt_v, True)
+    start_all(q2, SIDE)
+    pass_on(1)
+    pass_on(2)
+    pass_on(0)
+    recv_all(q2, SIDE)
+    finish_prefix(qr_v, qp_v, qz_v, qb_v, True)
+    t_v[me] = qb_v[me]
+    lax.fori_loop(0, HEADS, dq_head, 0, unroll=True)
+    put_q = pltpu.make_async_copy(q_v, dq_hbm, loc.at[5])
+    put_q.start()
+    for colour in range(3):
+        product(colour)
+    start_all(q3, PLANE)
     for colour in range(3):
         (lo, hi), _, axis, _ = COLOURS[colour]
         for d in (1, 3, 2):
@@ -411,7 +387,12 @@
             s3_v[i, :, lo:hi] = value.astype(BF16)
         for d in (1, 3, 2):
             s3_copy(colour, d).start()
-
+    recv_all(q3, PLANE)
+    lax.fori_loop(0, HEADS, kv_head, 0, unroll=True)
+    put_k = pltpu.make_async_copy(k_v, dk_hbm, loc.at[6])
+    put_v = pltpu.make_async_copy(v_v, dv_hbm, loc.at[7])
+    put_k.start()
+    put_v.start()
     for colour in range(3):
         (lo, hi), _, _, axis = COLOURS[colour]
         for d in (1, 3, 2):
@@ -441,6 +422,24 @@
         put.wait()
 
 
+def put_out(a, b, c, e, oa, ob, oc, oe, va, vb, vc, ve, into, out):
+    gets = [
+        pltpu.make_async_copy(s, v, into.at[i])
+        for i, (s, v) in enumerate(((a, va), (b, vb), (c, vc), (e, ve)))
+    ]
+    puts = [
+        pltpu.make_async_copy(v, o, out.at[i])
+        for i, (v, o) in enumerate(((va, oa), (vb, ob), (vc, oc), (ve, oe)))
+    ]
+    for get in gets:
+        get.start()
+    for get, put in zip(gets, puts):
+        get.wait()
+        put.start()
+    for put in puts:
+        put.wait()
+
+
 def local(queries, keys, values, out_weight, grad_out, doc_ids):
     total_rows = ROWS * lax.axis_size("ctx")
     factor = 1.0 / math.sqrt(HD * total_rows / DOCS)
@@ -461,7 +460,7 @@
         vm(*flat), vm(*flat), vm(*flat), vm(WIDTH, MODEL), vm(2, *flat), vm(*flat),
         vm(SIDE, SIDE, SIDE, BLOCK, ROWS),
         vm(ROWS, HD, dtype=F32), vm(ROWS, ROWS, dtype=F32), vm(HEADS, ROWS, ROWS),
-        vm(8, 128), vm(*flat, dtype=F32), vm(*flat, dtype=F32), vm(*flat, dtype=F32),
+        vm(*flat, dtype=F32), vm(*flat, dtype=F32), vm(*flat, dtype=F32),
         vm(*flat, dtype=F32), vm(BLOCK, HEADS, HD, dtype=F32),
         *prefix, *prefix,
         vm(3, SIDE, SIDE, SIDE, BLOCK, ROWS), vm(SIDE, *flat),
@@ -472,18 +471,28 @@
     ]
     any_space = pl.BlockSpec(memory_space=pl.ANY)
     shape = jax.ShapeDtypeStruct
-    return pl.pallas_call(
+    outs = (
+        shape(flat, BF16), shape(flat, BF16), shape(flat, BF16), shape((BLOCK, HEADS, HD), F32),
+    )
+    results = pl.pallas_call(
         lambda *refs: kernel(factor, weight_factor, *refs),
-        out_shape=(
-            shape(flat, BF16), shape(flat, BF16), shape(flat, BF16),
-            shape((BLOCK, HEADS, HD), F32),
-        ),
+        out_shape=outs,
         in_specs=[pl.BlockSpec(memory_space=pltpu.VMEM)] + [any_space] * 5,
         out_specs=(any_space,) * 4,
         scratch_shapes=scratch,
         compiler_params=pltpu.CompilerParams(collective_id=0, has_side_effects=True),
         name="linear_attention_backward",
     )(doc_ids.reshape(1, ROWS), queries, keys, values, out_weight, grad_out)
+    return pl.pallas_call(
+        put_out,
+        out_shape=outs,
+        in_specs=[any_space] * 4,
+        out_specs=(any_space,) * 4,
+        scratch_shapes=[
+            vm(*flat), vm(*flat), vm(*flat), vm(BLOCK, HEADS, HD, dtype=F32), dma((4,)), dma((4,)),
+        ],
+        name="results",
+    )(*results)
 
 
 def solution(mesh):

time: 63.4 us -> 54.5 us (0.86)
  local copies, waits for them, and re-layouts: 7.17 us -> 0 us
  Pallas kernels: 55.3 us -> 53.7 us
    unnamed x4 -> x0, local copies, waits for them, and re-layouts: 7.17 us -> none
    pallas_call x1, Pallas kernels: 55.3 us -> 51.5 us  [local(): pl.pallas_call(lambda *refs: kernel(factor, weight_factor, *refs), out_sh...]
    pallas_call x0 -> x1, Pallas kernels: none -> 2.28 us  [local(): pl.pallas_call(put_out, out_shape=outs, in_specs=[any_space] * 4, out_spe...]
where the time goes in v2:
time: 54.5 us; the launch traced here: 54.4 us
  Pallas kernels  53.7 us (99%)
  between operations  0.64 us (1%)
    pallas_call x1, Pallas kernels, local(): pl.pallas_call(lambda *refs: kernel(factor, weight_factor, *refs), out_sh...  51.5 us
    pallas_call x1, Pallas kernels, local(): pl.pallas_call(put_out, out_shape=outs, in_specs=[any_space] * 4, out_spe...  2.28 us

profile of v2, /device:TPU:0, one launch (start us, length us, event | category | flops | bytes accessed | tf_op | source)
XLA Modules:
  0.0 54.4 jit_solution(1164659013911451967)
XLA Ops:
  0.6 51.5 %linear_attention_backward.1 = (bf16[256,1024]{1,0:T(8,128)(2,1)}, bf16[256,1024]{1,0:T(8,128)(2,1)}, bf16[256,1024]{1,0:T(8,128)(2,1)}, f32[32,8,128]{2,1,0:T(8,128)}) custom-call(s32[1,256]{1,0:T(1,128)} %bitcast.1, bf16[256,1024]{1,0:T(8,128)(2,1)} %refs_1_.1, bf16[256,1024]{1,0:T(8,128)(2,1)} %refs_2_.1, bf16[256,1024]{1,0:T(8,128)(2,1)} %refs_3_.1, ...), custom_call_target="tpu_custom_call" | custom-call | tf_op jit(solution)/shard_map/linear_attention_backward/pallas_call | solution.py:477
  52.1 2.3 %results.1 = (bf16[256,1024]{1,0:T(8,128)(2,1)}, bf16[256,1024]{1,0:T(8,128)(2,1)}, bf16[256,1024]{1,0:T(8,128)(2,1)}, f32[32,8,128]{2,1,0:T(8,128)}) custom-call(bf16[256,1024]{1,0:T(8,128)(2,1)} %get-tuple-element.8.a, bf16[256,1024]{1,0:T(8,128)(2,1)} %get-tuple-element.9.b, bf16[256,1024]{1,0:T(8,128)(2,1)} %get-tuple-element.10.c, ...), custom_call_target="tpu_custom_call" | custom-call | tf_op jit(solution)/shard_map/results/pallas_call | solution.py:486

commit v3 on v2

--- a/solution.py
+++ b/solution.py
@@ -19,6 +19,9 @@
 BLOCK = 32
 MESH = pl.DeviceIdType.MESH
 COLOURS = (((0, 384), 0, 1, 2), ((384, 768), 1, 2, 0), ((768, 1024), 2, 0, 1))
+UNITS = (
+    (0, 0, 256), (1, 384, 640), (2, 768, 896), (0, 256, 384), (1, 640, 768), (2, 896, 1024),
+)
 F32 = jnp.float32
 BF16 = jnp.bfloat16
 
@@ -167,14 +170,15 @@
         total[0:PIECE, :] = acc.astype(BF16)
         total[PIECE:, :] = jnp.broadcast_to(mark, (16, HD)).astype(BF16)
 
-    def finish_prefix(recv, part, zrecv, back, backward):
+    def finish_prefix(recv, part, zrecv, back, backward, make=None):
         terms = []
         for d in (1, 2, 3):
             valid = (d > z) if backward else (d <= z)
             keep = jnp.where(valid, 1.0, 0.0)
             terms.append((zrecv[d, 0:PIECE, :].astype(F32) * keep, zrecv[d, PIECE:, :].astype(F32)[0:1]))
 
-        def one(m, carry):
+        def one(k, carry):
+            m = (me + k) % PLANE
             ids = recv[m, PIECE:, :].astype(F32)
             near = ids[8:9] if backward else ids[0:1]
             value = part[m]
@@ -183,7 +187,14 @@
             back[m] = value.astype(BF16)
             return carry
 
-        lax.fori_loop(0, PLANE, one, 0, unroll=True)
+        def both(k, carry):
+            one(k, carry)
+            if make is not None:
+                make(k).start()
+            return carry
+
+        lax.fori_loop(1, PLANE, both, 0, unroll=True)
+        one(0, 0)
 
     def flip(hf):
         def one(j, carry):
@@ -268,33 +279,38 @@
         part = gb_v.at[colour, d, pl.ds(2 * half, 2)]
         return remote(part, part, fs.at[colour, d], fr.at[colour, d], partner)
 
-    def a_copy(colour, d):
-        (lo, hi), axis = COLOURS[colour][:2]
+    def a_copy(unit, d):
+        colour, lo, hi = UNITS[unit]
+        axis = COLOURS[colour][1]
         return remote(
             ab_v.at[0, :, lo:hi], ab_v.at[d, :, lo:hi],
-            as_.at[colour, d], ar.at[colour, d], axis_peer(axis, d),
+            as_.at[unit, d], ar.at[unit, d], axis_peer(axis, d),
         )
 
-    def s2_copy(colour, d):
-        (lo, hi), _, axis, _ = COLOURS[colour]
+    def s2_copy(unit, d):
+        colour, lo, hi = UNITS[unit]
+        axis = COLOURS[colour][2]
         return remote(
             s2_v.at[(pos[axis] + d) % SIDE, :, lo:hi], r2_v.at[d, :, lo:hi],
-            b2s.at[colour, d], b2r.at[colour, d], axis_peer(axis, d),
+            b2s.at[unit, d], b2r.at[unit, d], axis_peer(axis, d),
         )
 
-    def s3_copy(colour, d):
-        (lo, hi), _, _, axis = COLOURS[colour]
+    def s3_copy(unit, d):
+        colour, lo, hi = UNITS[unit]
+        axis = COLOURS[colour][3]
         return remote(
             s3_v.at[(pos[axis] + d) % SIDE, :, lo:hi], r3_v.at[d, :, lo:hi],
-            b3s.at[colour, d], b3r.at[colour, d], axis_peer(axis, d),
+            b3s.at[unit, d], b3r.at[unit, d], axis_peer(axis, d),
         )
 
-    def product(colour):
-        (lo, hi), _, axis, _ = COLOURS[colour]
-        for d in (1, 3, 2):
-            g_pass(colour, d).wait_recv()
-        for d in (1, 3, 2):
-            a_copy(colour, d).wait_recv()
+    def product(unit):
+        colour, lo, hi = UNITS[unit]
+        axis = COLOURS[colour][2]
+        if unit < 3:
+            for d in (1, 3, 2):
+                g_pass(colour, d).wait_recv()
+        for d in (1, 3, 2):
+            a_copy(unit, d).wait_recv()
         for o in range(SIDE):
             value = dot(gb_v[colour, 0, o].reshape(128, ROWS), ab_v[0, :, lo:hi])
             for d in (1, 2, 3):
@@ -306,7 +322,7 @@
             else:
                 s2_v[o, :, lo:hi] = value
         for d in (1, 3, 2):
-            s2_copy(colour, d).start()
+            s2_copy(unit, d).start()
 
     def own_slices():
         gb_v[0, 0] = gt_v[z]
@@ -348,37 +364,37 @@
     send_g(0)
     own_slices()
     recv_all(k2, SIDE)
-    finish_prefix(kr_v, kp_v, kz_v, kb_v, False)
-    start_all(k3, PLANE)
+    finish_prefix(kr_v, kp_v, kz_v, kb_v, False, k3)
     s_v[me] = kb_v[me]
     start_all(q1, PLANE)
     lax.fori_loop(0, HEADS, pulled_head, 0, unroll=True)
 
     recv_all(k3, PLANE)
-    for colour in range(3):
-        lo, hi = COLOURS[colour][0]
+    for unit, (_, lo, hi) in enumerate(UNITS):
         lax.fori_loop(lo // HD, hi // HD, out_head, 0, unroll=True)
         for d in (1, 3, 2):
-            a_copy(colour, d).start()
+            a_copy(unit, d).start()
+    pass_on(1)
+    pass_on(2)
+    pass_on(0)
     recv_all(q1, PLANE)
     scan_plane(qr_v, qp_v, qt_v, True)
     start_all(q2, SIDE)
-    pass_on(1)
-    pass_on(2)
-    pass_on(0)
+    lax.fori_loop(0, HEADS, dq_head, 0, unroll=True)
+    put_q = pltpu.make_async_copy(q_v, dq_hbm, loc.at[5])
+    put_q.start()
+    for unit in range(3):
+        product(unit)
     recv_all(q2, SIDE)
     finish_prefix(qr_v, qp_v, qz_v, qb_v, True)
     t_v[me] = qb_v[me]
-    lax.fori_loop(0, HEADS, dq_head, 0, unroll=True)
-    put_q = pltpu.make_async_copy(q_v, dq_hbm, loc.at[5])
-    put_q.start()
-    for colour in range(3):
-        product(colour)
     start_all(q3, PLANE)
-    for colour in range(3):
-        (lo, hi), _, axis, _ = COLOURS[colour]
-        for d in (1, 3, 2):
-            s2_copy(colour, d).wait_recv()
+    for unit in range(3, len(UNITS)):
+        product(unit)
+    for unit, (colour, lo, hi) in enumerate(UNITS):
+        axis = COLOURS[colour][2]
+        for d in (1, 3, 2):
+            s2_copy(unit, d).wait_recv()
         for i in range(SIDE):
             rows = slice(i * BLOCK, (i + 1) * BLOCK)
             value = s2_v[pos[axis], rows, lo:hi].astype(F32)
@@ -386,17 +402,17 @@
                 value = value + r2_v[d, rows, lo:hi].astype(F32)
             s3_v[i, :, lo:hi] = value.astype(BF16)
         for d in (1, 3, 2):
-            s3_copy(colour, d).start()
+            s3_copy(unit, d).start()
     recv_all(q3, PLANE)
     lax.fori_loop(0, HEADS, kv_head, 0, unroll=True)
     put_k = pltpu.make_async_copy(k_v, dk_hbm, loc.at[6])
     put_v = pltpu.make_async_copy(v_v, dv_hbm, loc.at[7])
     put_k.start()
     put_v.start()
-    for colour in range(3):
-        (lo, hi), _, _, axis = COLOURS[colour]
-        for d in (1, 3, 2):
-            s3_copy(colour, d).wait_recv()
+    for unit, (colour, lo, hi) in enumerate(UNITS):
+        axis = COLOURS[colour][3]
+        for d in (1, 3, 2):
+            s3_copy(unit, d).wait_recv()
         value = s3_v[pos[axis], :, lo:hi].astype(F32)
         for d in (1, 2, 3):
             value = value + r3_v[d, :, lo:hi].astype(F32)
@@ -415,9 +431,11 @@
         for d in (1, 2, 3):
             g_copy(colour, d).wait_send()
             g_pass(colour, d).wait_send()
-            a_copy(colour, d).wait_send()
-            s2_copy(colour, d).wait_send()
-            s3_copy(colour, d).wait_send()
+    for unit in range(len(UNITS)):
+        for d in (1, 2, 3):
+            a_copy(unit, d).wait_send()
+            s2_copy(unit, d).wait_send()
+            s3_copy(unit, d).wait_send()
     for put in (put_q, put_k, put_v, put_w):
         put.wait()
 
@@ -467,7 +485,8 @@
         vm(SIDE, 128, WIDTH), vm(SIDE, 128, WIDTH), vm(SIDE, BLOCK, WIDTH), vm(SIDE, BLOCK, WIDTH),
         dma((9,)), dma(()), dma(()),
         *prefix_sems, *prefix_sems,
-        *[dma((3, SIDE)) for _ in range(10)],
+        *[dma((3, SIDE)) for _ in range(4)],
+        *[dma((len(UNITS), SIDE)) for _ in range(6)],
     ]
     any_space = pl.BlockSpec(memory_space=pl.ANY)
     shape = jax.ShapeDtypeStruct

time: 54.5 us -> 53.1 us (0.974)
  Pallas kernels: 53.7 us -> 52.3 us
    pallas_call x1, Pallas kernels: 51.5 us -> 50 us  [local(): pl.pallas_call(lambda *refs: kernel(factor, weight_factor, *refs), out_sh...]
where the time goes in v3:
time: 53.1 us; the launch traced here: 53 us
  Pallas kernels  52.3 us (98%)
  between operations  0.64 us (1%)
    pallas_call x1, Pallas kernels, local(): pl.pallas_call(lambda *refs: kernel(factor, weight_factor, *refs), out_sh...  50 us
    pallas_call x1, Pallas kernels, local(): pl.pallas_call(put_out, out_shape=outs, in_specs=[any_space] * 4, out_spe...  2.28 us

profile of v3, /device:TPU:0, one launch (start us, length us, event | category | flops | bytes accessed | tf_op | source)
XLA Modules:
  0.0 53.0 jit_solution(1149603194935640903)
XLA Ops:
  0.6 50.0 %linear_attention_backward.1 = (bf16[256,1024]{1,0:T(8,128)(2,1)}, bf16[256,1024]{1,0:T(8,128)(2,1)}, bf16[256,1024]{1,0:T(8,128)(2,1)}, f32[32,8,128]{2,1,0:T(8,128)}) custom-call(s32[1,256]{1,0:T(1,128)} %bitcast.1, bf16[256,1024]{1,0:T(8,128)(2,1)} %refs_1_.1, bf16[256,1024]{1,0:T(8,128)(2,1)} %refs_2_.1, bf16[256,1024]{1,0:T(8,128)(2,1)} %refs_3_.1, ...), custom_call_target="tpu_custom_call" | custom-call | tf_op jit(solution)/shard_map/linear_attention_backward/pallas_call | solution.py:496
  50.7 2.3 %results.1 = (bf16[256,1024]{1,0:T(8,128)(2,1)}, bf16[256,1024]{1,0:T(8,128)(2,1)}, bf16[256,1024]{1,0:T(8,128)(2,1)}, f32[32,8,128]{2,1,0:T(8,128)}) custom-call(bf16[256,1024]{1,0:T(8,128)(2,1)} %get-tuple-element.8.a, bf16[256,1024]{1,0:T(8,128)(2,1)} %get-tuple-element.9.b, bf16[256,1024]{1,0:T(8,128)(2,1)} %get-tuple-element.10.c, ...), custom_call_target="tpu_custom_call" | custom-call | tf_op jit(solution)/shard_map/results/pallas_call | solution.py:505
